TPU v7x, 32 devices: a whole 2x2x4 slice. The times are simulated.
32 devices in a mesh: seq: 8 (over z, x), vocab: 4 (over y, core).
Axes of the slice: x: 2, y: 2, z: 4, core: 2. Of those that a mesh axis runs over, the one named last changes fastest.
Arguments:
- rollout: bfloat16 [288, 4096], P('seq')
- group_count: int32 [8], replicated, may hold values from 12 to 36, as said below
- final_gain: float32 [4096], replicated, may hold values from 0.5 to 1.5
- head_weight: bfloat16 [4096, 152064], P(None, ('seq', 'vocab'))
- teacher_index: int32 [192, 64], replicated, may hold values from 0 to 152063, as said below
- teacher_logprob: float32 [192, 64], replicated, as said below
Outputs:
- kl: float32 [192], P('seq')
- grad_weight: bfloat16 [4096, 152064], P(None, ('seq', 'vocab'))
- grad_rollout: bfloat16 [288, 4096], P('seq', 'vocab')
Inputs may be any that keep to these rules, and one draw needn't show every extreme that they name: The first group_count[g] of the 36 slots of group g are live, the rest padding; the counts sum to 192. `teacher_index`: the 64 ids of one token are distinct. `teacher_logprob`: the exponentials of one token's entries sum to less than 1.
All inputs are finite; a program needn't handle non-finite values.
Results may differ from a plain program's by a relative error of at most 0.0075.
Values may be sent and summed in bfloat16 or wider, within the bound.
A program may use at most 128 MiB of HBM per device.

v0:
```python
import jax
import jax.numpy as jnp
from jax import lax
from jax.sharding import PartitionSpec as P

norm_eps = 1e-06
loss_scale = 16.0


def per_device(rollout, group_count, final_gain, head_weight, teacher_index, teacher_logprob):
    groups = lax.axis_size("seq")
    gen_slots, feature_width = rollout.shape
    tokens = teacher_index.shape[0]
    pack_rows = tokens // groups
    capacity = -(-gen_slots // groups)
    own_index = lax.axis_index("seq")
    offsets = jnp.cumsum(group_count) - group_count
    own_offset = offsets[own_index]
    own_count = group_count[own_index]
    row_ids = jnp.arange(capacity * groups, dtype=jnp.int32)
    padded = jnp.pad(rollout, ((0, capacity * groups - gen_slots), (0, 0)))
    padded = jnp.where((row_ids < own_count)[:, None], padded, jnp.zeros_like(padded))
    outgoing = jnp.roll(padded.reshape(capacity, groups, feature_width), own_offset, axis=1)
    arriving = lax.all_to_all(outgoing, "seq", split_axis=1, concat_axis=1, tiled=True)
    slot_ids = jnp.arange(capacity, dtype=jnp.int32)[:, None]
    row_in_group = slot_ids * groups + (own_index - offsets[None, :]) % groups
    is_live = row_in_group < group_count[None, :]
    position = jnp.where(is_live, (offsets[None, :] + row_in_group) // groups, pack_rows)
    packed = jnp.zeros((pack_rows, feature_width), rollout.dtype)
    packed = packed.at[position.reshape(-1)].set(arriving.reshape(-1, feature_width), mode="drop")
    values = packed.astype(jnp.float32)
    inv_rms = lax.rsqrt(jnp.mean(values * values, axis=1, keepdims=True) + norm_eps)
    normed = (values * inv_rms * final_gain).astype(jnp.bfloat16)
    all_rows = lax.all_gather(normed, "seq", axis=0, tiled=True)
    logits = jnp.dot(all_rows, head_weight, preferred_element_type=jnp.float32)
    vocab_dev = head_weight.shape[1]
    first_column = lax.axis_index(("seq", "vocab")) * vocab_dev
    local_index = teacher_index - first_column
    owned = (local_index >= 0) & (local_index < vocab_dev)
    teacher_prob = jnp.exp(teacher_logprob)
    teacher_mass = jnp.sum(teacher_prob, axis=1)
    token_ids = jnp.arange(tokens, dtype=jnp.int32)[:, None]
    column = jnp.where(owned, local_index, vocab_dev)
    teacher_dense = (
        jnp.zeros((tokens, vocab_dev), jnp.float32)
        .at[token_ids, column]
        .add(teacher_prob, mode="drop")
    )
    target_part = jnp.sum(teacher_dense * logits, axis=1)
    local_peak = jnp.max(logits, axis=1)
    row_peak = lax.pmax(local_peak, ("seq", "vocab"))
    local_total = jnp.sum(jnp.exp(logits - row_peak[:, None]), axis=1)
    row_total, target_sum = lax.psum((local_total, target_part), ("seq", "vocab"))
    log_total = row_peak + jnp.log(row_total)
    kl_all = jnp.sum(teacher_prob * teacher_logprob, axis=1) - target_sum + teacher_mass * log_total
    kl = lax.dynamic_slice_in_dim(kl_all, own_index * pack_rows, pack_rows)
    student_part = teacher_mass[:, None] * jnp.exp(logits - log_total[:, None]) - teacher_dense
    grad_logits = (loss_scale * student_part).astype(jnp.bfloat16)
    grad_weight = lax.dot_general(
        all_rows, grad_logits, (((0,), (0,)), ((), ())), preferred_element_type=jnp.float32
    ).astype(jnp.bfloat16)
    share = feature_width // lax.axis_size("vocab")
    feature_start = lax.axis_index("vocab") * share
    x_share = lax.dynamic_slice_in_dim(values, feature_start, share, 1)
    partial_rows = lax.psum_scatter(
        lax.dot_general(
            grad_logits, head_weight, (((1,), (1,)), ((), ())), preferred_element_type=jnp.float32
        ),
        "seq",
        scatter_dimension=0,
        tiled=True,
    )
    whole_rows = lax.psum(partial_rows, "vocab")
    full_grad = whole_rows * final_gain
    row_dots = jnp.sum(full_grad * values, axis=1, keepdims=True)
    scaled_grad = lax.dynamic_slice_in_dim(full_grad, feature_start, share, 1)
    grad_packed = (
        (scaled_grad - x_share * inv_rms * inv_rms * row_dots / feature_width) * inv_rms
    ).astype(jnp.bfloat16)
    taken = jnp.take(grad_packed, jnp.minimum(position, pack_rows - 1), axis=0)
    outgoing_back = jnp.where(is_live[:, :, None], taken, jnp.zeros_like(taken))
    coming_back = lax.all_to_all(outgoing_back, "seq", split_axis=1, concat_axis=1, tiled=True)
    restored = jnp.roll(coming_back, -own_offset, axis=1).reshape(capacity * groups, share)
    grad_rollout = restored[:gen_slots]
    return (kl, grad_weight, grad_rollout)


def solution(mesh):
    placed = (P("seq", None), P(), P(), P(None, ("seq", "vocab")), P(), P())
    return jax.shard_map(
        per_device,
        mesh=mesh,
        in_specs=placed,
        out_specs=(P("seq"), P(None, ("seq", "vocab")), P("seq", "vocab")),
        check_vma=False,
    )
```

profile of v0, /device:TPU:0, one launch (start us, length us, event | category | flops | bytes accessed | tf_op | source)
XLA Modules:
  0.0 382.8 jit_solution(6932193462676987082)
XLA Ops:
  7.2 1.3 dynamic_slice.23
  8.5 0.8 reduce-window.9
  9.3 0.7 and_select_fusion.1
  10.0 0.6 dynamic_slice.24
  12.5 0.7 iota_compare_fusion
  13.2 1.1 select_bitcast_fusion
  14.3 0.2 fusion.2
  14.6 1.0 copy.18
  15.5 7.3 %all-to-all-start = ((bf16[5,8,4096]{2,0,1:T(8,128)(2,1)}), bf16[5,8,4096]{2,0,1:T(8,128)(2,1)S(1)}, u32[]{:S(2)}, u32[]{:S(2)}) async-start(bf16[5,8,4096]{2,0,1:T(8,128)(2,1)} %copy.18), calls=%async_computation | async-start | bytes 1048576 | tf_op jit(solution)/shard_map/all_to_all | solution.py:24
  22.9 0.7 compare_and_fusion
  23.9 13.4 %all-to-all-done = bf16[5,8,4096]{2,0,1:T(8,128)(2,1)S(1)} async-done(((bf16[5,8,4096]{2,0,1:T(8,128)(2,1)}), bf16[5,8,4096]{2,0,1:T(8,128)(2,1)S(1)}, u32[]{:S(2)}, u32[]{:S(2)}) %all-to-all-start) | async-done | bytes 327712 | tf_op jit(solution)/shard_map/all_to_all | solution.py:24
  37.3 1.4 scatter_custom_fusion
  38.7 0.2 multiply_reduce_fusion.2
  38.9 0.8 multiply_convert_fusion.1
  39.9 0.1 and_reduce_fusion
  40.5 66.5 %scatter_custom_fusion.1 = f32[912384]{0:T(1024)} fusion(s32[12288]{0:T(1024)S(1)} %reshape.401, f32[12288]{0:T(1024)S(1)} %reshape.403, f32[]{:T(128)} %constant.100.clone.1), kind=kCustom, calls=%fused_computation.7 | custom fusion | flops 12288 | bytes 3649540
  107.0 5.8 %reshape.384 = f32[192,4752]{1,0:T(8,128)} reshape(f32[912384]{0:T(1024)} %scatter_custom_fusion.1) | data formatting | bytes 7299072 | tf_op jit(solution)/shard_map/scatter-add | solution.py:47
  112.7 20.6 %fusion.31 = (f32[192]{0:T(256)S(1)}, f32[192,4752]{1,0:T(8,128)}) fusion(bf16[192,4096]{1,0:T(8,128)(2,1)} %all-gather.2.cloned.1.call-done, bf16[4096,4752]{0,1:T(8,128)(2,1)} %param.9), kind=kOutput, calls=%fused_computation.86 | convolution fusion | flops 7475162112 | bytes 44151552 | tf_op jit(solution)/shard_map/dot_general | solution.py:35
  133.3 38.4 %pmax.7 = f32[192]{0:T(256)S(1)} all-reduce(f32[192]{0:T(256)S(1)} %get-tuple-element.18), channel_id=1, replica_groups=mesh['seq'=8,'vocab'=4] {'seq','vocab'}, use_global_device_ids=true, to_apply=%region_9.10 | all-reduce | flops 192 | bytes 1536 | tf_op jit(solution)/shard_map/pmax | solution.py:51
  171.7 4.2 %multiply_reduce_fusion = (f32[192]{0:T(256)S(1)}, f32[192]{0:T(256)S(1)}) fusion(f32[192,4752]{1,0:T(8,128)} %reshape.384, f32[192,4752]{1,0:T(8,128)} %get-tuple-element.19, f32[192]{0:T(256)S(1)} %pmax.7), kind=kLoop, calls=%fused_computation.6 | loop fusion | flops 3649152 | bytes 7301376 | tf_op jit(solution)/shard_map/reduce_sum | solution.py:49
  175.9 40.9 %all-reduce.1 = (f32[192]{0:T(256)S(1)}, f32[192]{0:T(256)S(1)}) all-reduce(f32[192]{0:T(256)S(1)} %get-tuple-element.4, f32[192]{0:T(256)S(1)} %get-tuple-element.3), channel_id=1, replica_groups=mesh['seq'=8,'vocab'=4] {'seq','vocab'}, use_global_device_ids=true, to_apply=%region_11.12 | all-reduce | flops 384 | bytes 3072 | tf_op jit(solution)/shard_map/psum | solution.py:53
  216.8 4.1 %multiply_convert_fusion = bf16[192,4752]{1,0:T(8,128)(2,1)S(1)} fusion(f32[192,4752]{1,0:T(8,128)} %reshape.384, f32[192,4752]{1,0:T(8,128)} %get-tuple-element.19, f32[192]{0:T(256)S(1)} %get-tuple-element.12, f32[192]{0:T(256)S(1)} %get-tuple-element.6), kind=kLoop, calls=%fused_computation.4 | loop fusion | flops 4561920 | bytes 9125376 | tf_op jit(solution)/shard_map/convert_element_type | solution.py:58
  220.9 18.2 %fusion.32 = f32[192,4096]{1,0:T(8,128)} fusion(bf16[192,4752]{1,0:T(8,128)(2,1)S(1)} %multiply_convert_fusion, bf16[4096,4752]{0,1:T(8,128)(2,1)} %param.9), kind=kOutput, calls=%fused_computation.87 | convolution fusion | flops 7474249728 | bytes 43898880 | tf_op jit(solution)/shard_map/dot_general | solution.py:66
  239.3 74.6 %reduce-scatter.2.cloned.1.call-done = f32[24,4096]{1,0:T(8,128)} async-done(((f32[192,4096]{1,0:T(8,128)}), f32[24,4096]{1,0:T(8,128)}) %reduce-scatter.2.cloned.1.call-update) | async-done | bytes 393232 | tf_op jit(solution)/shard_map/reduce_scatter | solution.py:65
  315.0 33.2 %all-reduce.4.cloned.1.call-done = f32[24,4096]{1,0:T(8,128)} async-done(((f32[24,4096]{1,0:T(8,128)}), f32[24,4096]{1,0:T(8,128)}) %all-reduce.4.cloned.1.call-update) | async-done | bytes 393232 | tf_op jit(solution)/shard_map/psum | solution.py:73
  348.2 1.2 multiply_reduce_fusion.1
  349.4 0.7 gather_fusion
  350.1 0.7 fusion.6
  350.8 5.5 %all-to-all-start.1 = ((bf16[5,8,1024]{2,0,1:T(8,128)(2,1)}), bf16[5,8,1024]{2,0,1:T(8,128)(2,1)S(1)}, u32[]{:S(2)}, u32[]{:S(2)}) async-start(bf16[5,8,1024]{2,0,1:T(8,128)(2,1)} %fusion.6), calls=%async_computation.2 | async-start | bytes 262144 | tf_op jit(solution)/shard_map/all_to_all | solution.py:82
  356.3 18.6 %convolution_convert_fusion = bf16[4096,4752]{0,1:T(8,128)(2,1)} fusion(bf16[192,4096]{1,0:T(8,128)(2,1)} %all-gather.2.cloned.1.call-done, bf16[192,4752]{1,0:T(8,128)(2,1)S(1)} %multiply_convert_fusion), kind=kOutput, calls=%fused_computation.3 | convolution fusion | flops 7493713920 | bytes 42326016 | tf_op jit(solution)/shard_map/dot_general | solution.py:59
  374.9 0.6 dynamic_slice.26
  375.6 0.7 fusion.9
  (44 shorter events, 1.5 us)
Async XLA Ops:
  7.2 32.7 %copy-start.5 = (s32[2]{0:T(128)S(1)}, s32[2]{0:T(128)}, u32[]{:S(2)}) copy-start(s32[2]{0:T(128)} %constant.127) | copy-start | bytes 28
  7.2 32.8 %copy-start.4 = (s32[2]{0:T(128)S(1)}, s32[2]{0:T(128)}, u32[]{:S(2)}) copy-start(s32[2]{0:T(128)} %constant.130) | copy-start | bytes 28
  7.2 31.7 %copy-start = (f32[4096]{0:T(1024)S(1)}, f32[4096]{0:T(1024)}, u32[]{:S(2)}) copy-start(f32[4096]{0:T(1024)} %param.8) | copy-start | bytes 49156
  7.2 32.6 %copy-start.1 = (s32[192,64]{0,1:T(8,128)S(1)}, s32[192,64]{0,1:T(8,128)}, u32[]{:S(2)}) copy-start(s32[192,64]{0,1:T(8,128)} %param.10) | copy-start | bytes 147460
  7.2 33.0 %copy-start.2 = (f32[192,64]{0,1:T(8,128)S(1)}, f32[192,64]{0,1:T(8,128)}, u32[]{:S(2)}) copy-start(f32[192,64]{0,1:T(8,128)} %param.11) | copy-start | bytes 147460
  15.5 21.8 %all-to-all-start = ((bf16[5,8,4096]{2,0,1:T(8,128)(2,1)}), bf16[5,8,4096]{2,0,1:T(8,128)(2,1)S(1)}, u32[]{:S(2)}, u32[]{:S(2)}) async-start(bf16[5,8,4096]{2,0,1:T(8,128)(2,1)} %copy.18), calls=%async_computation | async-start | bytes 1048576 | tf_op jit(solution)/shard_map/all_to_all | solution.py:24
  22.8 89.9 %all-gather.2.cloned.1.call-start = ((), (), s32[]{:S(2)}) async-start(), calls=%async_computation.3 | async-start | bytes 1769472 | tf_op jit(solution)/shard_map/all_gather | solution.py:34
  39.7 274.2 %reduce-scatter.2.cloned.1.call-start = ((), (), s32[]{:S(2)}) async-start(), calls=%async_computation.4 | async-start | bytes 3538944 | tf_op jit(solution)/shard_map/reduce_scatter | solution.py:65
  220.9 93.0 %copy-start.3 = (s32[8]{0:T(128)S(1)}, s32[8]{0:T(128)}, u32[]{:S(2)}) copy-start(s32[8]{0:T(128)} %param.7) | copy-start | bytes 100
  239.2 109.0 %all-reduce.4.cloned.1.call-start = ((), (), s32[]{:S(2)}) async-start(), calls=%async_computation.5 | async-start | bytes 786432 | tf_op jit(solution)/shard_map/psum | solution.py:73
  350.8 24.7 %all-to-all-start.1 = ((bf16[5,8,1024]{2,0,1:T(8,128)(2,1)}), bf16[5,8,1024]{2,0,1:T(8,128)(2,1)S(1)}, u32[]{:S(2)}, u32[]{:S(2)}) async-start(bf16[5,8,1024]{2,0,1:T(8,128)(2,1)} %fusion.6), calls=%async_computation.2 | async-start | bytes 262144 | tf_op jit(solution)/shard_map/all_to_all | solution.py:82
Sparse Core Ops, SparseCore 0:
  39.8 43.2 all-gather.1
  239.3 74.4 reduce-scatter.1
  316.2 31.8 all-reduce.3
where the time goes:
time: 384 us; the launch traced here: 383 us
  waiting for transfers between devices  121 us (32%)
  other arithmetic  83.2 us (22%)
  blocking collectives  79.3 us (21%)
  matrix products  57.5 us (15%)
  between operations  16.6 us (4%)
  starting transfers between devices  12.9 us (3%)
  local copies, waits for them, and re-layouts  12.1 us (3%)
    reduce_scatter x1, waiting for transfers between devices, per_device(): lax.psum_scatter(lax.dot_general(grad_logits, head_weight, (((1,), (1,)),...  74.6 us
    unnamed x4, other arithmetic  66.7 us
    psum x1, blocking collectives, per_device(): lax.psum((local_total, target_part), ('seq', 'vocab'))  40.9 us
    pmax x1, blocking collectives, per_device(): row_peak = lax.pmax(local_peak, ('seq', 'vocab'))  38.4 us
    psum x1, waiting for transfers between devices, per_device(): whole_rows = lax.psum(partial_rows, 'vocab')  33.2 us
    dot_general x1, matrix products, per_device(): logits = jnp.dot(all_rows, head_weight, preferred_element_type=jnp.float32)  20.6 us
    dot_general x1, matrix products, per_device(): lax.dot_general(all_rows, grad_logits, (((0,), (0,)), ((), ())), preferre...  18.6 us
    dot_general x1, matrix products, per_device(): lax.dot_general(grad_logits, head_weight, (((1,), (1,)), ((), ())), prefe...  18.2 us
  transfers between devices with their start and end apart: 5, of which 3 were waited for; matrix products, arithmetic and copies ran while one was open for 24% of the time, Pallas kernels for 0%

commit v1 on v0

--- a/solution.py
+++ b/solution.py
@@ -70,7 +70,7 @@
         scatter_dimension=0,
         tiled=True,
     )
-    whole_rows = lax.psum(partial_rows, "vocab")
+    whole_rows = jnp.sum(lax.all_gather(partial_rows, "vocab"), axis=0)
     full_grad = whole_rows * final_gain
     row_dots = jnp.sum(full_grad * values, axis=1, keepdims=True)
     scaled_grad = lax.dynamic_slice_in_dim(full_grad, feature_start, share, 1)

time: 384 us -> 370 us (0.964)
  waiting for transfers between devices: 121 us -> 107 us
    psum x1 -> x0, waiting for transfers between devices: 33.2 us -> none  [per_device(): whole_rows = lax.psum(partial_rows, 'vocab')]
    all_gather x0 -> x1, waiting for transfers between devices: none -> 19.2 us  [per_device(): whole_rows = jnp.sum(lax.all_gather(partial_rows, 'vocab'), axis=0)]
  transfers between devices with their start and end apart: 5 -> 5, of which waited for: 3 -> 3; matrix products, arithmetic and copies ran while one was open for 24% -> 25% of each run, Pallas kernels for 0% -> 0%
where the time goes in v1:
time: 370 us; the launch traced here: 369 us
  waiting for transfers between devices  107 us (29%)
  other arithmetic  83.7 us (23%)
  blocking collectives  79.3 us (21%)
  matrix products  57.5 us (16%)
  between operations  16.6 us (4%)
  starting transfers between devices  12.9 us (3%)
  local copies, waits for them, and re-layouts  12.1 us (3%)
    reduce_scatter x1, waiting for transfers between devices, per_device(): lax.psum_scatter(lax.dot_general(grad_logits, head_weight, (((1,), (1,)),...  74.6 us
    unnamed x4, other arithmetic  66.7 us
    psum x1, blocking collectives, per_device(): lax.psum((local_total, target_part), ('seq', 'vocab'))  40.9 us
    pmax x1, blocking collectives, per_device(): row_peak = lax.pmax(local_peak, ('seq', 'vocab'))  38.4 us
    dot_general x1, matrix products, per_device(): logits = jnp.dot(all_rows, head_weight, preferred_element_type=jnp.float32)  20.6 us
    all_gather x1, waiting for transfers between devices, per_device(): whole_rows = jnp.sum(lax.all_gather(partial_rows, 'vocab'), axis=0)  19.2 us
    dot_general x1, matrix products, per_device(): lax.dot_general(all_rows, grad_logits, (((0,), (0,)), ((), ())), preferre...  18.6 us
    dot_general x1, matrix products, per_device(): lax.dot_general(grad_logits, head_weight, (((1,), (1,)), ((), ())), prefe...  18.2 us
  transfers between devices with their start and end apart: 5, of which 3 were waited for; matrix products, arithmetic and copies ran while one was open for 25% of the time, Pallas kernels for 0%

profile of v1, /device:TPU:0, one launch (start us, length us, event | category | flops | bytes accessed | tf_op | source)
XLA Modules:
  0.0 369.4 jit_solution(4648988111076316867)
XLA Ops:
  7.2 1.3 dynamic_slice.23
  8.5 0.8 reduce-window.9
  9.3 0.7 and_select_fusion.1
  10.0 0.6 dynamic_slice.24
  12.5 0.7 iota_compare_fusion
  13.2 1.1 select_bitcast_fusion
  14.3 0.2 fusion.2
  14.6 1.0 copy.18
  15.5 7.3 %all-to-all-start = ((bf16[5,8,4096]{2,0,1:T(8,128)(2,1)}), bf16[5,8,4096]{2,0,1:T(8,128)(2,1)S(1)}, u32[]{:S(2)}, u32[]{:S(2)}) async-start(bf16[5,8,4096]{2,0,1:T(8,128)(2,1)} %copy.18), calls=%async_computation | async-start | bytes 1048576 | tf_op jit(solution)/shard_map/all_to_all | solution.py:24
  22.9 0.7 compare_and_fusion
  23.9 13.4 %all-to-all-done = bf16[5,8,4096]{2,0,1:T(8,128)(2,1)S(1)} async-done(((bf16[5,8,4096]{2,0,1:T(8,128)(2,1)}), bf16[5,8,4096]{2,0,1:T(8,128)(2,1)S(1)}, u32[]{:S(2)}, u32[]{:S(2)}) %all-to-all-start) | async-done | bytes 327712 | tf_op jit(solution)/shard_map/all_to_all | solution.py:24
  37.3 1.4 scatter_custom_fusion
  38.7 0.2 multiply_reduce_fusion.2
  38.9 0.8 multiply_convert_fusion.1
  40.5 66.5 %scatter_custom_fusion.1 = f32[912384]{0:T(1024)} fusion(s32[12288]{0:T(1024)S(1)} %reshape.401, f32[12288]{0:T(1024)S(1)} %reshape.403, f32[]{:T(128)} %constant.100.clone.1), kind=kCustom, calls=%fused_computation.7 | custom fusion | flops 12288 | bytes 3649540
  107.0 5.8 %reshape.384 = f32[192,4752]{1,0:T(8,128)} reshape(f32[912384]{0:T(1024)} %scatter_custom_fusion.1) | data formatting | bytes 7299072 | tf_op jit(solution)/shard_map/scatter-add | solution.py:47
  112.7 20.6 %fusion.31 = (f32[192]{0:T(256)S(1)}, f32[192,4752]{1,0:T(8,128)}) fusion(bf16[192,4096]{1,0:T(8,128)(2,1)} %all-gather.4.cloned.1.call-done, bf16[4096,4752]{0,1:T(8,128)(2,1)} %param.9), kind=kOutput, calls=%fused_computation.86 | convolution fusion | flops 7475162112 | bytes 44151552 | tf_op jit(solution)/shard_map/dot_general | solution.py:35
  133.3 38.4 %pmax.7 = f32[192]{0:T(256)S(1)} all-reduce(f32[192]{0:T(256)S(1)} %get-tuple-element.18), channel_id=1, replica_groups=mesh['seq'=8,'vocab'=4] {'seq','vocab'}, use_global_device_ids=true, to_apply=%region_9.10 | all-reduce | flops 192 | bytes 1536 | tf_op jit(solution)/shard_map/pmax | solution.py:51
  171.7 4.2 %multiply_reduce_fusion = (f32[192]{0:T(256)S(1)}, f32[192]{0:T(256)S(1)}) fusion(f32[192,4752]{1,0:T(8,128)} %reshape.384, f32[192,4752]{1,0:T(8,128)} %get-tuple-element.19, f32[192]{0:T(256)S(1)} %pmax.7), kind=kLoop, calls=%fused_computation.6 | loop fusion | flops 3649152 | bytes 7301376 | tf_op jit(solution)/shard_map/reduce_sum | solution.py:49
  175.9 40.9 %all-reduce.1 = (f32[192]{0:T(256)S(1)}, f32[192]{0:T(256)S(1)}) all-reduce(f32[192]{0:T(256)S(1)} %get-tuple-element.4, f32[192]{0:T(256)S(1)} %get-tuple-element.3), channel_id=1, replica_groups=mesh['seq'=8,'vocab'=4] {'seq','vocab'}, use_global_device_ids=true, to_apply=%region_11.12 | all-reduce | flops 384 | bytes 3072 | tf_op jit(solution)/shard_map/psum | solution.py:53
  216.8 4.1 %multiply_convert_fusion = bf16[192,4752]{1,0:T(8,128)(2,1)S(1)} fusion(f32[192,4752]{1,0:T(8,128)} %reshape.384, f32[192,4752]{1,0:T(8,128)} %get-tuple-element.19, f32[192]{0:T(256)S(1)} %get-tuple-element.12, f32[192]{0:T(256)S(1)} %get-tuple-element.6), kind=kLoop, calls=%fused_computation.4 | loop fusion | flops 4561920 | bytes 9125376 | tf_op jit(solution)/shard_map/convert_element_type | solution.py:58
  220.9 18.2 %fusion.32 = f32[192,4096]{1,0:T(8,128)} fusion(bf16[192,4752]{1,0:T(8,128)(2,1)S(1)} %multiply_convert_fusion, bf16[4096,4752]{0,1:T(8,128)(2,1)} %param.9), kind=kOutput, calls=%fused_computation.87 | convolution fusion | flops 7474249728 | bytes 43898880 | tf_op jit(solution)/shard_map/dot_general | solution.py:66
  239.3 74.6 %reduce-scatter.2.cloned.1.call-done = f32[24,4096]{1,0:T(8,128)} async-done(((f32[192,4096]{1,0:T(8,128)}), f32[24,4096]{1,0:T(8,128)}) %reduce-scatter.2.cloned.1.call-update) | async-done | bytes 393232 | tf_op jit(solution)/shard_map/reduce_scatter | solution.py:65
  315.0 19.2 %all-gather.6.cloned.1.call-done = f32[96,4096]{1,0:T(8,128)} async-done(((f32[24,4096]{1,0:T(8,128)}), f32[96,4096]{1,0:T(8,128)}) %all-gather.6.cloned.1.call-update) | async-done | bytes 1572880 | tf_op jit(solution)/shard_map/all_gather | solution.py:73
  334.2 1.5 reduce_sum.68
  335.7 0.2 multiply_reduce_fusion.1
  336.0 0.7 gather_fusion
  336.7 0.7 fusion.6
  337.4 5.5 %all-to-all-start.1 = ((bf16[5,8,1024]{2,0,1:T(8,128)(2,1)}), bf16[5,8,1024]{2,0,1:T(8,128)(2,1)S(1)}, u32[]{:S(2)}, u32[]{:S(2)}) async-start(bf16[5,8,1024]{2,0,1:T(8,128)(2,1)} %fusion.6), calls=%async_computation.2 | async-start | bytes 262144 | tf_op jit(solution)/shard_map/all_to_all | solution.py:82
  342.9 18.6 %convolution_convert_fusion = bf16[4096,4752]{0,1:T(8,128)(2,1)} fusion(bf16[192,4096]{1,0:T(8,128)(2,1)} %all-gather.4.cloned.1.call-done, bf16[192,4752]{1,0:T(8,128)(2,1)S(1)} %multiply_convert_fusion), kind=kOutput, calls=%fused_computation.3 | convolution fusion | flops 7493713920 | bytes 42326016 | tf_op jit(solution)/shard_map/dot_general | solution.py:59
  361.5 0.6 dynamic_slice.26
  362.2 0.7 fusion.9
  (45 shorter events, 1.6 us)
Async XLA Ops:
  7.2 32.7 %copy-start.5 = (s32[2]{0:T(128)S(1)}, s32[2]{0:T(128)}, u32[]{:S(2)}) copy-start(s32[2]{0:T(128)} %constant.127) | copy-start | bytes 28
  7.2 32.8 %copy-start.4 = (s32[2]{0:T(128)S(1)}, s32[2]{0:T(128)}, u32[]{:S(2)}) copy-start(s32[2]{0:T(128)} %constant.130) | copy-start | bytes 28
  7.2 31.7 %copy-start = (f32[4096]{0:T(1024)S(1)}, f32[4096]{0:T(1024)}, u32[]{:S(2)}) copy-start(f32[4096]{0:T(1024)} %param.8) | copy-start | bytes 49156
  7.2 32.6 %copy-start.1 = (s32[192,64]{0,1:T(8,128)S(1)}, s32[192,64]{0,1:T(8,128)}, u32[]{:S(2)}) copy-start(s32[192,64]{0,1:T(8,128)} %param.10) | copy-start | bytes 147460
  7.2 33.0 %copy-start.2 = (f32[192,64]{0,1:T(8,128)S(1)}, f32[192,64]{0,1:T(8,128)}, u32[]{:S(2)}) copy-start(f32[192,64]{0,1:T(8,128)} %param.11) | copy-start | bytes 147460
  15.5 21.8 %all-to-all-start = ((bf16[5,8,4096]{2,0,1:T(8,128)(2,1)}), bf16[5,8,4096]{2,0,1:T(8,128)(2,1)S(1)}, u32[]{:S(2)}, u32[]{:S(2)}) async-start(bf16[5,8,4096]{2,0,1:T(8,128)(2,1)} %copy.18), calls=%async_computation | async-start | bytes 1048576 | tf_op jit(solution)/shard_map/all_to_all | solution.py:24
  22.8 89.9 %all-gather.4.cloned.1.call-start = ((), (), s32[]{:S(2)}) async-start(), calls=%async_computation.3 | async-start | bytes 1769472 | tf_op jit(solution)/shard_map/all_gather | solution.py:34
  39.7 274.2 %reduce-scatter.2.cloned.1.call-start = ((), (), s32[]{:S(2)}) async-start(), calls=%async_computation.4 | async-start | bytes 3538944 | tf_op jit(solution)/shard_map/reduce_scatter | solution.py:65
  220.9 93.8 %copy-start.3 = (s32[8]{0:T(128)S(1)}, s32[8]{0:T(128)}, u32[]{:S(2)}) copy-start(s32[8]{0:T(128)} %param.7) | copy-start | bytes 100
  239.2 95.0 %all-gather.6.cloned.1.call-start = ((), (), s32[]{:S(2)}) async-start(), calls=%async_computation.5 | async-start | bytes 1966080 | tf_op jit(solution)/shard_map/all_gather | solution.py:73
  337.4 24.7 %all-to-all-start.1 = ((bf16[5,8,1024]{2,0,1:T(8,128)(2,1)}), bf16[5,8,1024]{2,0,1:T(8,128)(2,1)S(1)}, u32[]{:S(2)}, u32[]{:S(2)}) async-start(bf16[5,8,1024]{2,0,1:T(8,128)(2,1)} %fusion.6), calls=%async_computation.2 | async-start | bytes 262144 | tf_op jit(solution)/shard_map/all_to_all | solution.py:82
Sparse Core Ops, SparseCore 0:
  39.8 43.2 all-gather.3
  239.3 74.4 reduce-scatter.1
  315.4 18.7 all-gather.5
